TPU v7x, 32 devices: a whole 2x2x4 slice. The times are simulated.
32 devices in a mesh: groups: 2 (over y), space: 4 (over x, core), chan: 4 (over z).
Axes of the slice: x: 2, y: 2, z: 4, core: 2. Of those that a mesh axis runs over, the one named last changes fastest.
Arguments:
- volume: bfloat16 [32, 16, 256, 256], P(('groups', 'space'), 'chan'), parts along dimension 0, may hold values from -6 to 6
- weight: bfloat16 [8, 256, 256], P(None, 'space', 'chan'), may hold values from -0.125 to 0.125
- cotangent: bfloat16 [16, 8, 128, 256], P(('groups', 'space'), None, None, 'chan'), parts along dimension 0, may hold values from -6 to 6
Outputs:
- grad_volume: bfloat16 [32, 16, 256, 256], P(('groups', 'space'), 'chan'), parts along dimension 0
- grad_weight: float32 [16, 256, 256], P('groups', 'space', 'chan'), parts along dimension 0
There are 2 independent parts, one for each index of `groups`. A program takes and returns all parts, laid end to end along the dimension named above; an argument that names none is the same for every part. Nothing has to cross between parts.
All inputs are finite; a program needn't handle non-finite values.
Results may differ from a plain program's by a relative error of at most 0.0049.
Values may be sent and summed in bfloat16 or wider, within the bound.
A program may use at most 64 MiB of HBM per device.

v0:
```python
import jax
import jax.numpy as jnp
from jax import lax
from jax.sharding import PartitionSpec as P


def patch_rows(block):
    cells_x, cells_y, cells_z, in_chan = block.shape
    shaped = block.reshape(cells_x // 2, 2, cells_y // 2, 2, cells_z // 2, 2, in_chan)
    return shaped.transpose(0, 2, 4, 1, 3, 5, 6).reshape(-1, 8, in_chan)


def unpatch(rows, cells_x, cells_y, cells_z):
    in_chan = rows.shape[2]
    shaped = rows.reshape(cells_x // 2, cells_y // 2, cells_z // 2, 2, 2, 2, in_chan)
    return shaped.transpose(0, 3, 1, 4, 2, 5, 6).reshape(cells_x, cells_y, cells_z, in_chan)


def shards(volume, weight, cotangent):
    cells_x, cells_y, cells_z, in_chan = volume.shape
    patches = patch_rows(volume)
    out_rows = patches.shape[0]
    wide_w = lax.all_gather(weight, "chan", axis=2, tiled=True)
    cot_tiles = lax.all_to_all(cotangent, "chan", split_axis=1, concat_axis=3, tiled=True)
    out_chan = cot_tiles.shape[3]
    upstream = cot_tiles.reshape(out_rows, out_chan)
    whole_w = lax.all_gather(wide_w, "space", axis=1, tiled=True)
    pre_act = jnp.einsum("mkc,kco->mo", patches, whole_w, preferred_element_type=jnp.float32)
    squash = jax.nn.sigmoid(pre_act)
    slopes = squash * (1.0 + pre_act * (1.0 - squash))
    deltas = (upstream.astype(jnp.float32) * slopes).astype(jnp.bfloat16)
    grad_rows = jnp.einsum(
        "mo,kco->mkc", deltas, whole_w, preferred_element_type=jnp.float32
    ).astype(jnp.bfloat16)
    grad_volume = unpatch(grad_rows, cells_x, cells_y, cells_z)
    partial_w = jnp.einsum("mkc,mo->kco", patches, deltas, preferred_element_type=jnp.float32)
    by_chan = lax.psum_scatter(partial_w, "chan", scatter_dimension=2, tiled=True)
    owned_sum = lax.psum_scatter(by_chan, "space", scatter_dimension=1, tiled=True)
    grad_weight = owned_sum / out_rows
    return (grad_volume, grad_weight)


def solution(mesh):
    return jax.shard_map(
        shards,
        mesh=mesh,
        in_specs=(
            P(("groups", "space"), "chan", None, None),
            P(None, "space", "chan"),
            P(("groups", "space"), None, None, "chan"),
        ),
        out_specs=(P(("groups", "space"), "chan", None, None), P("groups", "space", "chan")),
        check_vma=False,
    )
```

profile of v0, /device:TPU:0, one launch (start us, length us, event | category | flops | bytes accessed | tf_op | source)
XLA Modules:
  0.0 125.6 jit_solution(15146380185082460627)
XLA Ops:
  7.2 0.0 copy-start.2
  7.2 0.0 copy-start
  7.2 0.0 all-gather.2.cloned.1.call-start
  7.2 1.2 copy.19
  8.4 17.4 %all_gather.6 = bf16[8,64,256]{1,0,2:T(8,128)(2,1)S(1)} all-gather(bf16[8,64,64]{1,0,2:T(8,128)(2,1)S(1)} %copy.19), channel_id=1, replica_groups=mesh['groups'=2,'space'=4,'chan'=4] {'chan'}, dimensions={2}, use_global_device_ids=true | all-gather | bytes 327680 | tf_op jit(solution)/shard_map/all_gather | solution.py:23
  25.8 1.0 copy.20
  26.8 0.0 all-gather.2.cloned.1.call-update
  26.9 0.0 copy-done.2
  26.9 0.7 copy.16
  27.6 5.4 %all-to-all-start = ((bf16[2,8,128,64]{2,3,0,1:T(8,128)(2,1)}), bf16[2,8,128,64]{2,3,0,1:T(8,128)(2,1)S(1)}, u32[]{:S(2)}, u32[]{:S(2)}) async-start(bf16[2,8,128,64]{2,3,0,1:T(8,128)(2,1)} %copy.16), calls=%async_computation | async-start | bytes 524288 | tf_op jit(solution)/shard_map/all_to_all | solution.py:24
  33.0 0.0 reduce-scatter.5.cloned.1.call-start
  33.0 0.0 copy-done
  33.0 2.2 %reshape.22 = bf16[2,2,2,2,128,2,256]{6,5,4,3,2,1,0:T(2,128)(2,1)} reshape(bf16[4,4,256,256]{3,2,1,0:T(8,128)(2,1)S(1)} %copy-done) | data formatting | bytes 4194304 | tf_op jit(solution)/shard_map/reshape | solution.py:9
  35.2 2.1 %copy.18 = bf16[2,2,128,2,2,2,256]{6,2,1,0,5,4,3:T(8,128)(2,1)S(1)} copy(bf16[2,2,128,2,2,2,256]{6,5,2,4,1,3,0:T(2,128)(2,1)} %bitcast.37) | data formatting | bytes 4194304 | tf_op jit(solution)/shard_map/transpose | solution.py:10
  37.3 2.4 %all-to-all-done = bf16[2,8,128,64]{2,3,0,1:T(8,128)(2,1)S(1)} async-done(((bf16[2,8,128,64]{2,3,0,1:T(8,128)(2,1)}), bf16[2,8,128,64]{2,3,0,1:T(8,128)(2,1)S(1)}, u32[]{:S(2)}, u32[]{:S(2)}) %all-to-all-start) | async-done | bytes 262176 | tf_op jit(solution)/shard_map/all_to_all | solution.py:24
  39.8 0.3 copy.30
  40.0 0.4 reshape.26
  40.5 1.0 copy.21
  41.4 4.0 %all-gather.2.cloned.1.call-done = bf16[8,256,256]{2,1,0:T(8,128)(2,1)} async-done(((bf16[8,64,256]{2,1,0:T(8,128)(2,1)}), bf16[8,256,256]{2,1,0:T(8,128)(2,1)}) %all-gather.2.cloned.1.call-update) | async-done | bytes 1048592 | tf_op jit(solution)/shard_map/all_gather | solution.py:27
  45.5 2.1 %fusion = bf16[512,256,1]{1,0,2:T(8,128)(2,1)S(1)} fusion(f32[512,256]{1,0:T(8,128)} %copy.21, bf16[512,8,256]{2,0,1:T(8,128)(2,1)S(1)} %bitcast.34, bf16[8,256,256]{2,1,0:T(8,128)(2,1)} %all-gather.2.cloned.1.call-done), kind=kOutput, calls=%fused_computation.5 | convolution fusion | flops 538050560 | bytes 3932160 | tf_op jit(solution)/shard_map/mkc,kco->mo/dot_general | solution.py:28
  47.6 2.0 %convolution_bitcast_fusion = f32[8,256,256]{1,2,0:T(8,128)} fusion(bf16[512,256,1]{1,0,2:T(8,128)(2,1)S(1)} %fusion, bf16[512,8,256]{2,0,1:T(8,128)(2,1)S(1)} %bitcast.35), kind=kOutput, calls=%fused_computation.1 | convolution fusion | flops 536870912 | bytes 4456448 | tf_op jit(solution)/shard_map/mkc,mo->kco/dot_general | solution.py:36
  49.7 0.0 reduce-scatter.5.cloned.1.call-update
  49.7 0.0 copy-start.1
  49.7 0.0 reduce-scatter.7.cloned.1.call-start
  49.7 43.7 %reduce-scatter.5.cloned.1.call-done = f32[8,256,64]{1,2,0:T(8,128)} async-done(((f32[8,256,256]{1,2,0:T(8,128)}), f32[8,256,64]{1,2,0:T(8,128)}) %reduce-scatter.5.cloned.1.call-update) | async-done | bytes 524304 | tf_op jit(solution)/shard_map/reduce_scatter | solution.py:37
  93.5 1.5 %copy.27 = f32[8,256,64]{2,0,1:T(8,128)S(1)} copy(f32[8,256,64]{1,2,0:T(8,128)} %reduce-scatter.5.cloned.1.call-done) | data formatting | bytes 1048576
  95.0 1.1 reshape.31
  96.0 0.0 reduce-scatter.7.cloned.1.call-update
  96.1 0.0 copy-done.1
  96.1 0.7 convolution_convert_fusion
  96.8 2.2 %copy.22 = bf16[2,2,2,2,128,2,256]{6,5,4,3,2,1,0:T(2,128)(2,1)S(1)} copy(bf16[2,2,2,2,128,2,256]{6,4,2,0,5,3,1:T(8,128)(2,1)S(1)} %bitcast.36) | data formatting | bytes 4194304 | tf_op jit(solution)/shard_map/transpose | solution.py:16
  99.0 2.2 %reshape.25 = bf16[4,4,256,256]{3,2,1,0:T(8,128)(2,1)} reshape(bf16[2,2,2,2,128,2,256]{6,5,4,3,2,1,0:T(2,128)(2,1)S(1)} %copy.22) | data formatting | bytes 4194304 | tf_op jit(solution)/shard_map/reshape | solution.py:16
  101.2 15.9 %reduce-scatter.7.cloned.1.call-done = f32[64,512]{1,0:T(8,128)} async-done(((f32[256,512]{1,0:T(8,128)}), f32[64,512]{1,0:T(8,128)}) %reduce-scatter.7.cloned.1.call-update) | async-done | bytes 131088
  117.1 1.0 reshape.32
  118.1 0.1 copy.28
  118.2 0.8 copy.24
  (1 shorter events, 0.0 us)
Async XLA Ops:
  7.2 19.7 %copy-start.2 = (bf16[2,8,128,64]{2,3,1,0:T(8,128)(2,1)S(1)}, bf16[2,8,128,64]{2,3,1,0:T(8,128)(2,1)}, u32[]{:S(2)}) copy-start(bf16[2,8,128,64]{2,3,1,0:T(8,128)(2,1)} %param.5) | copy-start | bytes 786436
  7.2 25.8 %copy-start = (bf16[4,4,256,256]{3,2,1,0:T(8,128)(2,1)S(1)}, bf16[4,4,256,256]{3,2,1,0:T(8,128)(2,1)}, u32[]{:S(2)}) copy-start(bf16[4,4,256,256]{3,2,1,0:T(8,128)(2,1)} %param.3) | copy-start | bytes 6291460
  7.2 38.3 %all-gather.2.cloned.1.call-start = ((), (), s32[]{:S(2)}) async-start(), calls=%async_computation.3 | async-start | bytes 1310720 | tf_op jit(solution)/shard_map/all_gather | solution.py:27
  27.6 12.2 %all-to-all-start = ((bf16[2,8,128,64]{2,3,0,1:T(8,128)(2,1)}), bf16[2,8,128,64]{2,3,0,1:T(8,128)(2,1)S(1)}, u32[]{:S(2)}, u32[]{:S(2)}) async-start(bf16[2,8,128,64]{2,3,0,1:T(8,128)(2,1)} %copy.16), calls=%async_computation | async-start | bytes 524288 | tf_op jit(solution)/shard_map/all_to_all | solution.py:24
  33.0 60.5 %reduce-scatter.5.cloned.1.call-start = ((), (), s32[]{:S(2)}) async-start(), calls=%async_computation.4 | async-start | bytes 2621440 | tf_op jit(solution)/shard_map/reduce_scatter | solution.py:37
  49.7 46.4 %copy-start.1 = (bf16[8,256,256]{2,1,0:T(8,128)(2,1)S(1)}, bf16[8,256,256]{2,1,0:T(8,128)(2,1)}, u32[]{:S(2)}) copy-start(bf16[8,256,256]{2,1,0:T(8,128)(2,1)} %all-gather.2.cloned.1.call-done) | copy-start | bytes 3145732
  49.7 67.4 %reduce-scatter.7.cloned.1.call-start = ((), (), s32[]{:S(2)}) async-start(), calls=%async_computation.5 | async-start | bytes 655360
Sparse Core Ops, SparseCore 0:
  27.0 18.4 all-gather.1
  49.8 43.6 reduce-scatter.4
  96.2 20.8 reduce-scatter.6
where the time goes:
time: 126 us
  waiting for transfers between devices  66.1 us (52%)
  local copies, waits for them, and re-layouts  17.9 us (14%)
  blocking collectives  17.4 us (14%)
  between operations  13.9 us (11%)
  starting transfers between devices  5.47 us (4%)
  matrix products  4.93 us (4%)
    reduce_scatter x1, waiting for transfers between devices, shards(): lax.psum_scatter(partial_w, 'chan', scatter_dimension=2, tiled=True)  43.7 us
    all_gather x1, blocking collectives, shards(): wide_w = lax.all_gather(weight, 'chan', axis=2, tiled=True)  17.4 us
    unnamed x4, waiting for transfers between devices  15.9 us
    unnamed x13, local copies, waits for them, and re-layouts  6.45 us
    all_to_all x1, starting transfers between devices, shards(): lax.all_to_all(cotangent, 'chan', split_axis=1, concat_axis=3, tiled=True)  5.38 us
    all_gather x1, waiting for transfers between devices, shards(): whole_w = lax.all_gather(wide_w, 'space', axis=1, tiled=True)  4.02 us
  transfers between devices with their start and end apart: 4, of which 4 were waited for; matrix products, arithmetic and copies ran while one was open for 9% of the time, Pallas kernels for 0%

commit v1 on v0

--- a/solution.py
+++ b/solution.py
@@ -24,7 +24,8 @@
     cot_tiles = lax.all_to_all(cotangent, "chan", split_axis=1, concat_axis=3, tiled=True)
     out_chan = cot_tiles.shape[3]
     upstream = cot_tiles.reshape(out_rows, out_chan)
-    whole_w = lax.all_gather(wide_w, "space", axis=1, tiled=True)
+    terms = lax.all_gather(wide_w, "space", axis=0, tiled=False)
+    whole_w = jnp.concatenate(terms, axis=1)
     pre_act = jnp.einsum("mkc,kco->mo", patches, whole_w, preferred_element_type=jnp.float32)
     squash = jax.nn.sigmoid(pre_act)
     slopes = squash * (1.0 + pre_act * (1.0 - squash))

time: 126 us -> 126 us (level)
  matrix products: 4.93 us -> 3.57 us
  local copies, waits for them, and re-layouts: 17.9 us -> 19.2 us
    dot_general x1, matrix products: 2.13 us -> 0.78 us  [shards(): jnp.einsum('mkc,kco->mo', patches, whole_w, preferred_element_type=jnp.fl...]
    all_gather x0 -> x1, local copies, waits for them, and re-layouts: none -> 1.35 us  [shards(): terms = lax.all_gather(wide_w, 'space', axis=0, tiled=False)]
where the time goes in v1:
time: 126 us
  waiting for transfers between devices  66.1 us (52%)
  local copies, waits for them, and re-layouts  19.2 us (15%)
  blocking collectives  17.4 us (14%)
  between operations  13.8 us (11%)
  starting transfers between devices  5.47 us (4%)
  matrix products  3.57 us (3%)
    reduce_scatter x1, waiting for transfers between devices, shards(): lax.psum_scatter(partial_w, 'chan', scatter_dimension=2, tiled=True)  43.7 us
    all_gather x1, blocking collectives, shards(): wide_w = lax.all_gather(weight, 'chan', axis=2, tiled=True)  17.4 us
    unnamed x4, waiting for transfers between devices  15.9 us
    unnamed x13, local copies, waits for them, and re-layouts  6.44 us
    all_to_all x1, starting transfers between devices, shards(): lax.all_to_all(cotangent, 'chan', split_axis=1, concat_axis=3, tiled=True)  5.38 us
    all_gather x1, waiting for transfers between devices, shards(): terms = lax.all_gather(wide_w, 'space', axis=0, tiled=False)  4.02 us
  transfers between devices with their start and end apart: 4, of which 4 were waited for; matrix products, arithmetic and copies ran while one was open for 9% of the time, Pallas kernels for 0%

profile of v1, /device:TPU:0, one launch (start us, length us, event | category | flops | bytes accessed | tf_op | source)
XLA Modules:
  0.0 125.6 jit_solution(16790328148949751141)
XLA Ops:
  7.2 0.0 copy-start.2
  7.2 0.0 copy-start
  7.2 0.0 all-gather.3.cloned.1.call-start
  7.2 1.2 copy.21
  8.4 17.4 %all_gather.9 = bf16[8,64,256]{1,0,2:T(8,128)(2,1)S(1)} all-gather(bf16[8,64,64]{1,0,2:T(8,128)(2,1)S(1)} %copy.21), channel_id=1, replica_groups=mesh['groups'=2,'space'=4,'chan'=4] {'chan'}, dimensions={2}, use_global_device_ids=true | all-gather | bytes 327680 | tf_op jit(solution)/shard_map/all_gather | solution.py:23
  25.8 1.0 copy.22
  26.8 0.0 all-gather.3.cloned.1.call-update
  26.9 0.0 copy-done.2
  26.9 0.7 copy.18
  27.6 5.4 %all-to-all-start = ((bf16[2,8,128,64]{2,3,0,1:T(8,128)(2,1)}), bf16[2,8,128,64]{2,3,0,1:T(8,128)(2,1)S(1)}, u32[]{:S(2)}, u32[]{:S(2)}) async-start(bf16[2,8,128,64]{2,3,0,1:T(8,128)(2,1)} %copy.18), calls=%async_computation | async-start | bytes 524288 | tf_op jit(solution)/shard_map/all_to_all | solution.py:24
  33.0 0.0 reduce-scatter.5.cloned.1.call-start
  33.0 0.0 copy-done
  33.0 2.2 %reshape.28 = bf16[2,2,2,2,128,2,256]{6,5,4,3,2,1,0:T(2,128)(2,1)} reshape(bf16[4,4,256,256]{3,2,1,0:T(8,128)(2,1)S(1)} %copy-done) | data formatting | bytes 4194304 | tf_op jit(solution)/shard_map/reshape | solution.py:9
  35.2 2.1 %copy.20 = bf16[2,2,128,2,2,2,256]{6,2,1,0,5,4,3:T(8,128)(2,1)S(1)} copy(bf16[2,2,128,2,2,2,256]{6,5,2,4,1,3,0:T(2,128)(2,1)} %bitcast.41) | data formatting | bytes 4194304 | tf_op jit(solution)/shard_map/transpose | solution.py:10
  37.3 2.4 %all-to-all-done = bf16[2,8,128,64]{2,3,0,1:T(8,128)(2,1)S(1)} async-done(((bf16[2,8,128,64]{2,3,0,1:T(8,128)(2,1)}), bf16[2,8,128,64]{2,3,0,1:T(8,128)(2,1)S(1)}, u32[]{:S(2)}, u32[]{:S(2)}) %all-to-all-start) | async-done | bytes 262176 | tf_op jit(solution)/shard_map/all_to_all | solution.py:24
  39.8 0.3 copy.33
  40.0 0.4 reshape.34
  40.5 1.0 copy.24
  41.4 4.0 %all-gather.3.cloned.1.call-done = bf16[32,64,256]{2,1,0:T(8,128)(2,1)} async-done(((bf16[8,64,256]{2,1,0:T(8,128)(2,1)}), bf16[32,64,256]{2,1,0:T(8,128)(2,1)}) %all-gather.3.cloned.1.call-update) | async-done | bytes 1048592 | tf_op jit(solution)/shard_map/all_gather | solution.py:27
  45.5 0.0 copy-start.1
  45.5 1.4 %copy.23 = bf16[4,8,64,256]{3,2,0,1:T(8,128)(2,1)S(1)} copy(bf16[4,8,64,256]{3,2,1,0:T(8,128)(2,1)} %bitcast.47) | data formatting | bytes 2097152 | tf_op jit(solution)/shard_map/all_gather | solution.py:27
  46.8 0.0 copy-done.1
  46.8 0.8 fusion
  47.6 2.0 %convolution_bitcast_fusion = f32[8,256,256]{1,2,0:T(8,128)} fusion(bf16[512,256,1]{1,0,2:T(8,128)(2,1)S(1)} %fusion, bf16[512,8,256]{2,0,1:T(8,128)(2,1)S(1)} %bitcast.39), kind=kOutput, calls=%fused_computation.1 | convolution fusion | flops 536870912 | bytes 4456448 | tf_op jit(solution)/shard_map/mkc,mo->kco/dot_general | solution.py:37
  49.7 0.0 reduce-scatter.5.cloned.1.call-update
  49.7 0.0 reduce-scatter.7.cloned.1.call-start
  49.7 43.7 %reduce-scatter.5.cloned.1.call-done = f32[8,256,64]{1,2,0:T(8,128)} async-done(((f32[8,256,256]{1,2,0:T(8,128)}), f32[8,256,64]{1,2,0:T(8,128)}) %reduce-scatter.5.cloned.1.call-update) | async-done | bytes 524304 | tf_op jit(solution)/shard_map/reduce_scatter | solution.py:38
  93.5 1.5 %copy.30 = f32[8,256,64]{2,0,1:T(8,128)S(1)} copy(f32[8,256,64]{1,2,0:T(8,128)} %reduce-scatter.5.cloned.1.call-done) | data formatting | bytes 1048576
  95.0 1.1 reshape.40
  96.0 0.0 reduce-scatter.7.cloned.1.call-update
  96.1 0.7 convolution_convert_fusion
  96.8 2.2 %copy.25 = bf16[2,2,2,2,128,2,256]{6,5,4,3,2,1,0:T(2,128)(2,1)S(1)} copy(bf16[2,2,2,2,128,2,256]{6,4,2,0,5,3,1:T(8,128)(2,1)S(1)} %bitcast.40) | data formatting | bytes 4194304 | tf_op jit(solution)/shard_map/transpose | solution.py:16
  99.0 2.2 %reshape.33 = bf16[4,4,256,256]{3,2,1,0:T(8,128)(2,1)} reshape(bf16[2,2,2,2,128,2,256]{6,5,4,3,2,1,0:T(2,128)(2,1)S(1)} %copy.25) | data formatting | bytes 4194304 | tf_op jit(solution)/shard_map/reshape | solution.py:16
  101.2 15.8 %reduce-scatter.7.cloned.1.call-done = f32[64,512]{1,0:T(8,128)} async-done(((f32[256,512]{1,0:T(8,128)}), f32[64,512]{1,0:T(8,128)}) %reduce-scatter.7.cloned.1.call-update) | async-done | bytes 131088
  117.0 1.0 reshape.41
  118.0 0.1 copy.31
  118.2 0.8 copy.27
  (1 shorter events, 0.0 us)
Async XLA Ops:
  7.2 19.7 %copy-start.2 = (bf16[2,8,128,64]{2,3,1,0:T(8,128)(2,1)S(1)}, bf16[2,8,128,64]{2,3,1,0:T(8,128)(2,1)}, u32[]{:S(2)}) copy-start(bf16[2,8,128,64]{2,3,1,0:T(8,128)(2,1)} %param.5) | copy-start | bytes 786436
  7.2 25.8 %copy-start = (bf16[4,4,256,256]{3,2,1,0:T(8,128)(2,1)S(1)}, bf16[4,4,256,256]{3,2,1,0:T(8,128)(2,1)}, u32[]{:S(2)}) copy-start(bf16[4,4,256,256]{3,2,1,0:T(8,128)(2,1)} %param.3) | copy-start | bytes 6291460
  7.2 38.3 %all-gather.3.cloned.1.call-start = ((), (), s32[]{:S(2)}) async-start(), calls=%async_computation.4 | async-start | bytes 1310720 | tf_op jit(solution)/shard_map/all_gather | solution.py:27
  27.6 12.2 %all-to-all-start = ((bf16[2,8,128,64]{2,3,0,1:T(8,128)(2,1)}), bf16[2,8,128,64]{2,3,0,1:T(8,128)(2,1)S(1)}, u32[]{:S(2)}, u32[]{:S(2)}) async-start(bf16[2,8,128,64]{2,3,0,1:T(8,128)(2,1)} %copy.18), calls=%async_computation | async-start | bytes 524288 | tf_op jit(solution)/shard_map/all_to_all | solution.py:24
  33.0 60.5 %reduce-scatter.5.cloned.1.call-start = ((), (), s32[]{:S(2)}) async-start(), calls=%async_computation.3 | async-start | bytes 2621440 | tf_op jit(solution)/shard_map/reduce_scatter | solution.py:38
  45.5 1.4 %copy-start.1 = (f32[512,256]{1,0:T(8,128)S(1)}, f32[512,256]{1,0:T(8,128)}, u32[]{:S(2)}) copy-start(f32[512,256]{1,0:T(8,128)} %copy.24) | copy-start | bytes 1572868
  49.7 67.3 %reduce-scatter.7.cloned.1.call-start = ((), (), s32[]{:S(2)}) async-start(), calls=%async_computation.5 | async-start | bytes 655360
Sparse Core Ops, SparseCore 0:
  27.0 18.4 all-gather.2
  49.8 43.6 reduce-scatter.4
  96.2 20.8 reduce-scatter.6
